TPU v7x, 32 devices: a whole 2x2x4 slice. The times are simulated.
32 devices in a mesh: groups: 2 (over x), seq: 16 (over z, y, core).
Axes of the slice: x: 2, y: 2, z: 4, core: 2. Of those that a mesh axis runs over, the one named last changes fastest.
Arguments:
- images: bfloat16 [4, 2048, 3072], P('groups', 'seq'), parts along dimension 0, may hold values from -6 to 6
- w_qkv: bfloat16 [3072, 1152], replicated, may hold values from -0.109375 to 0.109375
- b_qkv: float32 [1152], replicated, may hold values from -3 to 3
- q_gain: float32 [128], replicated, may hold values from 0.5 to 2.5
- k_gain: float32 [128], replicated, may hold values from 0.5 to 2.5
- key_basis: float32 [3, 128, 32], replicated, may hold values from -0.5 to 0.5
- value_basis: float32 [3, 128, 32], replicated, may hold values from -0.5 to 0.5
- centers: float32 [4, 2, 3, 128], P('groups'), parts along dimension 0, may hold values from -22 to 22
- refresh: int32 [2, 3], replicated, may hold values 0 or 1
- w_out: bfloat16 [384, 3072], replicated, may hold values from -0.3125 to 0.3125
Outputs:
- mixed: bfloat16 [4, 2048, 3072], P('groups', 'seq'), parts along dimension 0
- new_centers: float32 [4, 2, 3, 128], P('groups'), parts along dimension 0
There are 2 independent parts, one for each index of `groups`. A program takes and returns all parts, laid end to end along the dimension named above; an argument that names none is the same for every part. Nothing has to cross between parts.
All inputs are finite; a program needn't handle non-finite values.
Results may differ from a plain program's by a relative error of at most 0.0051.
Values may be sent and summed in bfloat16 or wider, within the bound.
A program may use at most 64 MiB of HBM per device.

v0:
```python
import math
import jax
import jax.numpy as jnp
from jax import lax
from jax.sharding import PartitionSpec as P

epsilon = 1e-06
highest = lax.Precision.HIGHEST


def normalize(values, gain):
    mean_square = jnp.mean(values * values, axis=-1, keepdims=True)
    return values * lax.rsqrt(mean_square + epsilon) * gain


def per_device(
    images, w_qkv, b_qkv, q_gain, k_gain, key_basis, value_basis, centers, refresh, w_out
):
    sample_count, tokens_dev, model_width = images.shape
    head_count, head_dim, code_rank = key_basis.shape
    seq_count = lax.axis_size("seq")
    first_row = lax.axis_index("seq") * tokens_dev
    factor = 1.0 / math.sqrt(head_dim)
    flat_images = images.reshape(sample_count * tokens_dev, model_width)
    projected = jnp.dot(flat_images, w_qkv, preferred_element_type=jnp.float32) + b_qkv
    projected = projected.reshape(sample_count, tokens_dev, 3, head_count, head_dim)
    queries = normalize(projected[:, :, 0], q_gain)
    keys_local = normalize(projected[:, :, 1], k_gain)
    values_local = projected[:, :, 2]
    key_center = centers[:, 0]
    value_center = centers[:, 1]
    key_codes = jnp.einsum(
        "bthd,hdr->bthr", keys_local - key_center[:, None], key_basis, precision=highest
    ).astype(jnp.bfloat16)
    value_codes = jnp.einsum(
        "bthd,hdr->bthr", values_local - value_center[:, None], value_basis, precision=highest
    ).astype(jnp.bfloat16)
    local_sums = jnp.stack([jnp.sum(keys_local, axis=1), jnp.sum(values_local, axis=1)], axis=1)
    summed = lax.psum(local_sums, "seq")
    fresh_means = summed / (tokens_dev * seq_count)
    new_centers = jnp.where(refresh[None, :, :, None] == 1, fresh_means, centers)
    query_heads = queries.transpose(0, 2, 1, 3)
    key_heads = keys_local.transpose(0, 2, 1, 3)
    value_heads = values_local.transpose(0, 2, 1, 3)
    near_scores = jnp.einsum("bhqd,bhsd->bhqs", query_heads, key_heads, precision=highest) * factor
    start_max = jnp.max(near_scores, axis=-1)
    near_weights = jnp.exp(near_scores - start_max[..., None])
    start_sum = jnp.sum(near_weights, axis=-1)
    start_weighted = jnp.einsum("bhqs,bhsd->bhqd", near_weights, value_heads, precision=highest)
    packed = jnp.stack([key_codes, value_codes], axis=2)
    packed = packed.transpose(1, 0, 2, 3, 4).reshape(
        tokens_dev, sample_count, 2 * head_count * code_rank
    )

    def absorb(running, code_block, owned, low_sample, high_sample):
        row_max, row_sum, weighted = running
        block_values = code_block.astype(jnp.float32)
        key_part = block_values[:, :, 0]
        value_part = block_values[:, :, 1]
        key_rebuilt = (
            jnp.einsum("sbhr,hdr->bhsd", key_part, key_basis, precision=highest)
            + key_center[low_sample:high_sample, :, None, :]
        )
        scores = jnp.einsum("bhqd,bhsd->bhqs", query_heads, key_rebuilt, precision=highest) * factor
        scores = jnp.where(owned[None, None, None, :], -jnp.inf, scores)
        new_max = jnp.maximum(row_max, jnp.max(scores, axis=-1))
        fading = jnp.exp(row_max - new_max)
        weights = jnp.exp(scores - new_max[..., None])
        weight_sum = jnp.sum(weights, axis=-1)
        value_rebuilt = (
            jnp.einsum("sbhr,hdr->bhsd", value_part, value_basis, precision=highest)
            + value_center[low_sample:high_sample, :, None, :]
        )
        addition = jnp.einsum("bhqs,bhsd->bhqd", weights, value_rebuilt, precision=highest)
        return (new_max, row_sum * fading + weight_sum, weighted * fading[..., None] + addition)

    start_state = (start_max, start_sum, start_weighted)
    whole_codes = packed.reshape(tokens_dev, sample_count * 2 * head_count * code_rank)
    shard_codes = lax.all_gather(whole_codes, "seq", axis=0, tiled=True)
    row_count = shard_codes.shape[0]
    code_block = shard_codes.reshape(row_count, sample_count - 0, 2, head_count, code_rank)
    positions = jnp.arange(row_count, dtype=jnp.int32)
    owned = (positions >= first_row) & (positions < first_row + tokens_dev)
    block_rows = 512
    block_count = row_count // block_rows

    def advance(inner, blocks):
        return (absorb(inner, blocks[0], blocks[1], 0, sample_count), None)

    stacked = (
        code_block.reshape(block_count, block_rows, sample_count - 0, 2, head_count, code_rank),
        owned.reshape(block_count, block_rows),
    )
    result, unused = lax.scan(advance, start_state, stacked)
    final_max, final_sum, final_weighted = result
    attended = (final_weighted / final_sum[..., None]).transpose(0, 2, 1, 3)
    attended = attended.reshape(sample_count * tokens_dev, head_count * head_dim).astype(
        jnp.bfloat16
    )
    mixed = jnp.dot(attended, w_out, preferred_element_type=jnp.float32).astype(jnp.bfloat16)
    return (mixed.reshape(sample_count, tokens_dev, model_width), new_centers)


def solution(mesh):
    return jax.shard_map(
        per_device,
        mesh=mesh,
        in_specs=(
            P("groups", "seq", None),
            P(),
            P(),
            P(),
            P(),
            P(),
            P(),
            P("groups", None, None, None),
            P(),
            P(),
        ),
        out_specs=(P("groups", "seq", None), P("groups", None, None, None)),
        check_vma=False,
    )
```

profile of v0, /device:TPU:0, one launch (start us, length us, event | category | flops | bytes accessed | tf_op | source)
XLA Modules:
  0.0 120.0 jit_solution(16905698591683552414)
XLA Ops:
  7.2 0.0 copy-start
  7.2 0.0 all-gather.2.cloned.1.call-start
  7.2 5.8 %convolution_add_fusion = f32[256,1152]{1,0:T(8,128)S(1)} fusion(bf16[256,3072]{1,0:T(8,128)(2,1)} %bitcast.143, bf16[3072,1152]{1,0:T(8,128)(2,1)} %param.13, f32[1152]{0:T(1024)} %param.14), kind=kOutput, calls=%fused_computation.24 | convolution fusion | flops 1812234240 | bytes 9835008 | tf_op jit(solution)/shard_map/dot_general | solution.py:25
  13.0 1.4 %copy.42 = f32[256,1152]{0,1:T(8,128)} copy(f32[256,1152]{1,0:T(8,128)S(1)} %convolution_add_fusion) | data formatting | bytes 2359296 | tf_op jit(solution)/shard_map/add | solution.py:25
  14.4 1.9 %reshape.48 = f32[2,128,3,3,128]{1,0,4,3,2:T(2,128)S(1)} reshape(f32[256,1152]{0,1:T(8,128)} %copy.42) | data formatting | bytes 2359296 | tf_op jit(solution)/shard_map/reshape | solution.py:26
  16.3 0.0 copy-start.11
  16.3 0.9 multiply_reduce_fusion
  17.2 1.8 %slice_reduce_fusion = (f32[2,3,128]{0,2,1:T(8,128)}, f32[2,128,1,3,128]{1,0,4,3,2:T(2,128)}) fusion(f32[2,128,3,3,128]{1,0,4,3,2:T(2,128)S(1)} %reshape.48), kind=kLoop, calls=%fused_computation.64 | loop fusion | flops 97536 | bytes 789504 | tf_op jit(solution)/shard_map/reduce_sum | solution.py:38
  18.9 1.9 %copy.64 = f32[2,128,1,3,128]{4,1,3,0,2:T(8,128)} copy(f32[2,128,1,3,128]{1,0,4,3,2:T(2,128)} %get-tuple-element.119) | data formatting | bytes 786432
  20.8 0.0 copy-done.11
  20.9 0.8 copy.48
  21.7 0.7 add_rsqrt_fusion
  22.4 0.0 copy-start.1
  22.4 0.0 copy-start.5
  22.5 2.6 %fusion.32 = (f32[2,3,128]{0,2,1:T(8,128)}, f32[2,128,3,128]{1,0,3,2:T(2,128)S(1)}, f32[2,3,128,128]{2,0,3,1:T(2,128)}) fusion(f32[128]{0:T(128)} %param.16, f32[2,128,3]{1,0,2:T(2,128)S(1)} %get-tuple-element.129, f32[2,128,3,3,128]{1,0,4,3,2:T(2,128)S(1)} %reshape.48, f32[128]{0:T(128)} %param.15, f32[2,128,3]{1,0,2:T(2,128)S(1)} %get-tuple-element.130), kind=kLoop, calls=%fused_computation.65 | loop fusion | flops 490752 | bytes 1583104 | tf_op jit(solution)/shard_map/reduce_sum | solution.py:38
  25.0 0.5 broadcast_subtract_fusion
  25.5 0.3 fusion.15
  25.9 0.5 fusion.16
  26.4 0.6 copy.52
  27.1 0.0 all-gather.2.cloned.1.call-update
  27.1 1.2 copy.43
  28.3 1.6 %copy.56 = f32[2,3,128]{2,0,1:T(2,128)} copy(f32[2,3,128]{0,2,1:T(8,128)} %get-tuple-element.114) | data formatting | bytes 6144 | tf_op jit(solution)/shard_map/reduce_sum | solution.py:38
  29.9 1.6 %copy.57 = f32[2,3,128]{2,0,1:T(2,128)} copy(f32[2,3,128]{0,2,1:T(8,128)} %get-tuple-element.118) | data formatting | bytes 6144 | tf_op jit(solution)/shard_map/reduce_sum | solution.py:38
  31.5 0.7 pad_maximum_fusion
  32.2 36.5 %psum.7 = f32[2,2,3,128]{3,0,2,1:T(2,128)} all-reduce(f32[2,2,3,128]{3,0,2,1:T(2,128)S(1)} %pad_maximum_fusion), channel_id=1, replica_groups=mesh['groups'=2,'seq'=16] {'seq'}, use_global_device_ids=true, to_apply=%region_10.11 | all-reduce | flops 1536 | bytes 12288 | tf_op jit(solution)/shard_map/psum | solution.py:39
  68.7 0.7 broadcast_compare_fusion
  69.4 0.8 copy_select_fusion
  70.2 0.6 copy.59
  70.8 0.6 fusion.31
  71.4 0.8 fusion.36
  72.2 0.1 fusion.22
  72.3 0.8 fusion.17
  73.1 0.0 all-gather.2.cloned.1.call-done
  73.2 3.9 %reshape_reshape.7 = bf16[4,512,2,2,3,32]{1,0,5,4,3,2:T(4,128)(2,1)} reshape(bf16[2048,384]{0,1:T(8,128)(2,1)} %all-gather.2.cloned.1.call-done) | data formatting | bytes 3145728 | tf_op jit(solution)/shard_map/reshape;reshape | solution.py:91
  77.0 2.9 %copy.53 = bf16[4,512,2,2,3,32]{1,5,4,2,3,0:T(8,128)(2,1)} copy(bf16[4,512,2,2,3,32]{1,0,5,4,3,2:T(4,128)(2,1)} %reshape_reshape.7) | data formatting | bytes 3145728 | tf_op jit(solution)/shard_map/while | solution.py:94
  80.0 30.7 %while.14 = (s32[]{:T(128)}, f32[2,3,128]{2,1,0:T(4,128)S(1)}, f32[2,3,128]{2,1,0:T(4,128)S(1)}, f32[2,3,128,128]{3,2,1,0:T(8,128)S(1)}, pred[4,512]{1,0:T(4,128...) while((s32[]{:T(128)}, f32[2,3,128]{2,1,0:T(4,128)S(1)}, ...), condition=%wide.region_7.8_spmd, body=%wide.region_4.7_spmd.sunk | while | flops 1513293312 | bytes 13524605 | solution.py:94
  80.0 1.0 dynamic-slice_bitcast_fusion.2
  81.0 0.9 fusion.54
  81.9 1.6 %bitcast_reduce_fusion.2 = (f32[2,3,128]{2,1,0:T(4,128)S(1)}, f32[2,3,512,128]{3,2,1,0:T(8,128)S(1)}) fusion(f32[2,3,128,128]{3,2,1,0:T(8,128)S(1)} %get-tuple-element.240, f32[3,512,2,128]{3,1,0,2:T(8,128)S(1)} %fusion.54, f32[2,3,128]{2,1,0:T(4,128)S(1)} %bitcast.140, pred[512]{0:T(512)(128)(4,1)S(1)} %dynamic-slice_reduce_fusion.2), kind=kOutput, calls=%fused_computation.3.clone.1 | convolution fusion | flops 605551872 | bytes 3545600 | tf_op jit(solution)/shard_map/while/body/eval_jaxpr/bhqd,bhsd->bhqs/dot_general | solution.py:64
  83.6 0.2 fusion.55
  83.9 0.9 fusion.56
  84.8 2.9 %fusion.57 = f32[2,3,128,128]{3,2,1,0:T(8,128)S(1)} fusion(f32[3,512,2,128]{3,1,0,2:T(8,128)S(1)} %fusion.56, f32[2,3,512,128]{3,2,1,0:T(8,128)S(1)} %get-tuple-element.205, f32[2,3,128]{2,1,0:T(4,128)S(1)} %bitcast.139, f32[2,3,128]{2,1,0:T(4,128)S(1)} %max.4, f32[2,3,128,128]{3,2,1,0:T(8,128)S(1)} %get-tuple-element.223, ...), kind=kOutput, calls=%fused_computation.9.clone.1 | convolution fusion | flops 604962816 | bytes 3941376 | tf_op jit(solution)/shard_map/while/body/eval_jaxpr/bhqs,bhsd->bhqd/dot_general | solution.py:74
  87.7 1.0 dynamic-slice_bitcast_fusion.2
  88.7 0.9 fusion.54
  89.6 1.6 %bitcast_reduce_fusion.2 = (f32[2,3,128]{2,1,0:T(4,128)S(1)}, f32[2,3,512,128]{3,2,1,0:T(8,128)S(1)}) fusion(f32[2,3,128,128]{3,2,1,0:T(8,128)S(1)} %get-tuple-element.240, f32[3,512,2,128]{3,1,0,2:T(8,128)S(1)} %fusion.54, f32[2,3,128]{2,1,0:T(4,128)S(1)} %bitcast.140, pred[512]{0:T(512)(128)(4,1)S(1)} %dynamic-slice_reduce_fusion.2), kind=kOutput, calls=%fused_computation.3.clone.1 | convolution fusion | flops 605551872 | bytes 3545600 | tf_op jit(solution)/shard_map/while/body/eval_jaxpr/bhqd,bhsd->bhqs/dot_general | solution.py:64
  91.3 0.2 fusion.55
  91.5 0.9 fusion.56
  92.4 2.9 %fusion.57 = f32[2,3,128,128]{3,2,1,0:T(8,128)S(1)} fusion(f32[3,512,2,128]{3,1,0,2:T(8,128)S(1)} %fusion.56, f32[2,3,512,128]{3,2,1,0:T(8,128)S(1)} %get-tuple-element.205, f32[2,3,128]{2,1,0:T(4,128)S(1)} %bitcast.139, f32[2,3,128]{2,1,0:T(4,128)S(1)} %max.4, f32[2,3,128,128]{3,2,1,0:T(8,128)S(1)} %get-tuple-element.223, ...), kind=kOutput, calls=%fused_computation.9.clone.1 | convolution fusion | flops 604962816 | bytes 3941376 | tf_op jit(solution)/shard_map/while/body/eval_jaxpr/bhqs,bhsd->bhqd/dot_general | solution.py:74
  95.3 1.0 dynamic-slice_bitcast_fusion.2
  96.4 0.9 fusion.54
  97.3 1.6 %bitcast_reduce_fusion.2 = (f32[2,3,128]{2,1,0:T(4,128)S(1)}, f32[2,3,512,128]{3,2,1,0:T(8,128)S(1)}) fusion(f32[2,3,128,128]{3,2,1,0:T(8,128)S(1)} %get-tuple-element.240, f32[3,512,2,128]{3,1,0,2:T(8,128)S(1)} %fusion.54, f32[2,3,128]{2,1,0:T(4,128)S(1)} %bitcast.140, pred[512]{0:T(512)(128)(4,1)S(1)} %dynamic-slice_reduce_fusion.2), kind=kOutput, calls=%fused_computation.3.clone.1 | convolution fusion | flops 605551872 | bytes 3545600 | tf_op jit(solution)/shard_map/while/body/eval_jaxpr/bhqd,bhsd->bhqs/dot_general | solution.py:64
  98.9 0.2 fusion.55
  99.2 0.9 fusion.56
  100.1 2.9 %fusion.57 = f32[2,3,128,128]{3,2,1,0:T(8,128)S(1)} fusion(f32[3,512,2,128]{3,1,0,2:T(8,128)S(1)} %fusion.56, f32[2,3,512,128]{3,2,1,0:T(8,128)S(1)} %get-tuple-element.205, f32[2,3,128]{2,1,0:T(4,128)S(1)} %bitcast.139, f32[2,3,128]{2,1,0:T(4,128)S(1)} %max.4, f32[2,3,128,128]{3,2,1,0:T(8,128)S(1)} %get-tuple-element.223, ...), kind=kOutput, calls=%fused_computation.9.clone.1 | convolution fusion | flops 604962816 | bytes 3941376 | tf_op jit(solution)/shard_map/while/body/eval_jaxpr/bhqs,bhsd->bhqd/dot_general | solution.py:74
  103.0 1.0 dynamic-slice_bitcast_fusion.2
  104.0 0.9 fusion.54
  105.0 1.6 %bitcast_reduce_fusion.2 = (f32[2,3,128]{2,1,0:T(4,128)S(1)}, f32[2,3,512,128]{3,2,1,0:T(8,128)S(1)}) fusion(f32[2,3,128,128]{3,2,1,0:T(8,128)S(1)} %get-tuple-element.240, f32[3,512,2,128]{3,1,0,2:T(8,128)S(1)} %fusion.54, f32[2,3,128]{2,1,0:T(4,128)S(1)} %bitcast.140, pred[512]{0:T(512)(128)(4,1)S(1)} %dynamic-slice_reduce_fusion.2), kind=kOutput, calls=%fused_computation.3.clone.1 | convolution fusion | flops 605551872 | bytes 3545600 | tf_op jit(solution)/shard_map/while/body/eval_jaxpr/bhqd,bhsd->bhqs/dot_general | solution.py:64
  106.6 0.2 fusion.55
  106.9 0.9 fusion.56
  107.8 2.9 %fusion.57 = f32[2,3,128,128]{3,2,1,0:T(8,128)S(1)} fusion(f32[3,512,2,128]{3,1,0,2:T(8,128)S(1)} %fusion.56, f32[2,3,512,128]{3,2,1,0:T(8,128)S(1)} %get-tuple-element.205, f32[2,3,128]{2,1,0:T(4,128)S(1)} %bitcast.139, f32[2,3,128]{2,1,0:T(4,128)S(1)} %max.4, f32[2,3,128,128]{3,2,1,0:T(8,128)S(1)} %get-tuple-element.223, ...), kind=kOutput, calls=%fused_computation.9.clone.1 | convolution fusion | flops 604962816 | bytes 3941376 | tf_op jit(solution)/shard_map/while/body/eval_jaxpr/bhqs,bhsd->bhqd/dot_general | solution.py:74
  110.7 0.2 fusion.26
  110.8 0.2 copy.55
  111.0 0.0 copy-done
  111.0 2.2 %convolution_convert_fusion = bf16[256,3072]{1,0:T(8,128)(2,1)} fusion(bf16[384,3072]{1,0:T(8,128)(2,1)S(1)} %copy-done, bf16[48,8,2,128]{3,2,1,0:T(2,128)(2,1)S(1)} %bitcast.137), kind=kOutput, calls=%fused_computation.23 | convolution fusion | flops 604766208 | bytes 4128768 | tf_op jit(solution)/shard_map/dot_general | solution.py:100
  (37 shorter events, 0.3 us)
Async XLA Ops:
  7.2 103.9 %copy-start = (bf16[384,3072]{1,0:T(8,128)(2,1)S(1)}, bf16[384,3072]{1,0:T(8,128)(2,1)}, u32[]{:S(2)}) copy-start(bf16[384,3072]{1,0:T(8,128)(2,1)} %param.21) | copy-start | bytes 7077892
  7.2 66.0 %all-gather.2.cloned.1.call-start = ((), (), s32[]{:S(2)}) async-start(), calls=%async_computation | async-start | bytes 1671168 | tf_op jit(solution)/shard_map/all_gather | solution.py:79
  16.3 4.6 %copy-start.11 = (f32[2,2,3,128]{3,1,2,0:T(2,128)S(1)}, f32[2,2,3,128]{3,1,2,0:T(2,128)}, u32[]{:S(2)}) copy-start(f32[2,2,3,128]{3,1,2,0:T(2,128)} %param.19) | copy-start | bytes 18436
  21.7 3.3 %copy-start.9 = (f32[2,3,128]{0,2,1:T(8,128)S(1)}, f32[2,3,128]{0,2,1:T(8,128)}, u32[]{:S(2)}) copy-start(f32[2,3,128]{0,2,1:T(8,128)} %copy.48) | copy-start | bytes 9220
  21.7 3.8 %copy-start.7 = (f32[3,128,32]{1,2,0:T(8,128)S(1)}, f32[3,128,32]{1,2,0:T(8,128)}, u32[]{:S(2)}) copy-start(f32[3,128,32]{1,2,0:T(8,128)} %param.17) | copy-start | bytes 147460
  22.4 3.4 %copy-start.1 = (f32[2,128,1,3,128]{4,1,3,0,2:T(8,128)S(1)}, f32[2,128,1,3,128]{4,1,3,0,2:T(8,128)}, u32[]{:S(2)}) copy-start(f32[2,128,1,3,128]{4,1,3,0,2:T(8,128)} %copy.64) | copy-start | bytes 1179652
  22.4 3.4 %copy-start.5 = (f32[3,128,32]{1,2,0:T(8,128)S(1)}, f32[3,128,32]{1,2,0:T(8,128)}, u32[]{:S(2)}) copy-start(f32[3,128,32]{1,2,0:T(8,128)} %param.18) | copy-start | bytes 147460
  25.0 1.4 %copy-start.3 = (f32[2,128,3,128]{1,0,3,2:T(2,128)}, f32[2,128,3,128]{1,0,3,2:T(2,128)S(1)}, u32[]{:S(2)}) copy-start(f32[2,128,3,128]{1,0,3,2:T(2,128)S(1)} %get-tuple-element.115) | copy-start | bytes 1179652
  26.4 45.0 %copy-start.4 = (f32[2,128,3,128]{1,0,3,2:T(2,128)S(1)}, f32[2,128,3,128]{1,0,3,2:T(2,128)}, u32[]{:S(2)}) copy-start(f32[2,128,3,128]{1,0,3,2:T(2,128)} %copy-done.3) | copy-start | bytes 1179652
  26.4 45.9 %copy-start.2 = (f32[2,128,1,3,128]{4,1,3,0,2:T(8,128)S(1)}, f32[2,128,1,3,128]{4,1,3,0,2:T(8,128)}, u32[]{:S(2)}) copy-start(f32[2,128,1,3,128]{4,1,3,0,2:T(8,128)} %copy.64) | copy-start | bytes 1179652
  77.0 2.9 %copy-start.6 = (f32[3,128,32]{1,2,0:T(8,128)S(1)}, f32[3,128,32]{1,2,0:T(8,128)}, u32[]{:S(2)}) copy-start(f32[3,128,32]{1,2,0:T(8,128)} %param.18) | copy-start | bytes 147460
  77.0 2.9 %copy-start.8 = (f32[3,128,32]{1,2,0:T(8,128)S(1)}, f32[3,128,32]{1,2,0:T(8,128)}, u32[]{:S(2)}) copy-start(f32[3,128,32]{1,2,0:T(8,128)} %param.17) | copy-start | bytes 147460
  77.0 2.9 %copy-start.10 = (pred[4,512]{1,0:T(4,128)(4,1)S(1)}, pred[4,512]{1,0:T(4,128)(4,1)}, u32[]{:S(2)}) copy-start(pred[4,512]{1,0:T(4,128)(4,1)} %fusion.31) | copy-start | bytes 6148
Sparse Core Ops, SparseCore 0:
  27.2 41.7 all-gather.1
where the time goes:
time: 121 us; the launch traced here: 120 us
  blocking collectives  36.5 us (30%)
  matrix products  35.6 us (29%)
  local copies, waits for them, and re-layouts  22.8 us (19%)
  between operations  14.3 us (12%)
  other arithmetic  10.5 us (9%)
    psum x1, blocking collectives, per_device(): summed = lax.psum(local_sums, 'seq')  36.5 us
    dot_general x4, matrix products, absorb(): jnp.einsum('bhqs,bhsd->bhqd', weights, value_rebuilt, precision=highest)  11.5 us
    dot_general x4, matrix products, absorb(): jnp.einsum('bhqd,bhsd->bhqs', query_heads, key_rebuilt, precision=highest)  6.57 us
    dot_general x1, matrix products, per_device(): jnp.dot(flat_images, w_qkv, preferred_element_type=jnp.float32) + b_qkv  5.77 us
    squeeze x4, local copies, waits for them, and re-layouts, per_device(): result, unused = lax.scan(advance, start_state, stacked)  4.1 us
    another operation x1, local copies, waits for them, and re-layouts, per_device(): code_block.reshape(block_count, block_rows, sample_count - 0, 2, head_cou...  3.85 us
    dot_general x4, matrix products, absorb(): jnp.einsum('sbhr,hdr->bhsd', key_part, key_basis, precision=highest)  3.58 us
    dot_general x4, matrix products, absorb(): jnp.einsum('sbhr,hdr->bhsd', value_part, value_basis, precision=highest)  3.56 us
  transfers between devices with their start and end apart: 1, of which 0 were waited for; matrix products, arithmetic and copies ran while one was open for 8% of the time, Pallas kernels for 0%

commit v1 on v0

--- a/solution.py
+++ b/solution.py
@@ -36,7 +36,7 @@
         "bthd,hdr->bthr", values_local - value_center[:, None], value_basis, precision=highest
     ).astype(jnp.bfloat16)
     local_sums = jnp.stack([jnp.sum(keys_local, axis=1), jnp.sum(values_local, axis=1)], axis=1)
-    summed = lax.psum(local_sums, "seq")
+    summed = jnp.sum(lax.all_gather(local_sums, "seq"), axis=0)
     fresh_means = summed / (tokens_dev * seq_count)
     new_centers = jnp.where(refresh[None, :, :, None] == 1, fresh_means, centers)
     query_heads = queries.transpose(0, 2, 1, 3)

time: 121 us -> 116 us (0.959)
  blocking collectives: 36.5 us -> 25.1 us
  waiting for transfers between devices: 0.04 us -> 6.75 us
    psum x1 -> x0, blocking collectives: 36.5 us -> none  [per_device(): summed = lax.psum(local_sums, 'seq')]
    all_gather x0 -> x1, blocking collectives: none -> 25.1 us  [per_device(): summed = jnp.sum(lax.all_gather(local_sums, 'seq'), axis=0)]
    all_gather x1, waiting for transfers between devices: 0.02 us -> 6.73 us  [per_device(): shard_codes = lax.all_gather(whole_codes, 'seq', axis=0, tiled=True)]
    reduce_sum x2 -> x0, local copies, waits for them, and re-layouts: 3.22 us -> none  [the longest x1 1.61 us: per_device(): jnp.sum(keys_local, axis=1)]
    another operation x0 -> x2, local copies, waits for them, and re-layouts: none -> 1.62 us  [per_device(): jnp.stack([jnp.sum(keys_local, axis=1), jnp.sum(values_local, axis=1)], a...]
    unnamed x27 -> x28, local copies, waits for them, and re-layouts: 2.56 us -> 3.59 us
  transfers between devices with their start and end apart: 1 -> 1, of which waited for: 0 -> 1; matrix products, arithmetic and copies ran while one was open for 8% -> 9% of each run, Pallas kernels for 0% -> 0%
where the time goes in v1:
time: 116 us
  matrix products  35.6 us (31%)
  blocking collectives  25.1 us (22%)
  local copies, waits for them, and re-layouts  22.3 us (19%)
  between operations  14.2 us (12%)
  other arithmetic  11.4 us (10%)
  waiting for transfers between devices  6.75 us (6%)
    all_gather x1, blocking collectives, per_device(): summed = jnp.sum(lax.all_gather(local_sums, 'seq'), axis=0)  25.1 us
    dot_general x4, matrix products, absorb(): jnp.einsum('bhqs,bhsd->bhqd', weights, value_rebuilt, precision=highest)  11.5 us
    all_gather x1, waiting for transfers between devices, per_device(): shard_codes = lax.all_gather(whole_codes, 'seq', axis=0, tiled=True)  6.73 us
    dot_general x4, matrix products, absorb(): jnp.einsum('bhqd,bhsd->bhqs', query_heads, key_rebuilt, precision=highest)  6.58 us
    dot_general x1, matrix products, per_device(): jnp.dot(flat_images, w_qkv, preferred_element_type=jnp.float32) + b_qkv  5.77 us
    squeeze x4, local copies, waits for them, and re-layouts, per_device(): result, unused = lax.scan(advance, start_state, stacked)  4.1 us
    another operation x1, local copies, waits for them, and re-layouts, per_device(): code_block.reshape(block_count, block_rows, sample_count - 0, 2, head_cou...  3.85 us
    unnamed x28, local copies, waits for them, and re-layouts  3.59 us
  transfers between devices with their start and end apart: 1, of which 1 were waited for; matrix products, arithmetic and copies ran while one was open for 9% of the time, Pallas kernels for 0%

profile of v1, /device:TPU:0, one launch (start us, length us, event | category | flops | bytes accessed | tf_op | source)
XLA Modules:
  0.0 115.7 jit_solution(16703067394438944353)
XLA Ops:
  7.2 0.0 copy-start
  7.2 0.0 all-gather.3.cloned.1.call-start
  7.2 5.8 %convolution_add_fusion = f32[256,1152]{1,0:T(8,128)S(1)} fusion(bf16[256,3072]{1,0:T(8,128)(2,1)} %bitcast.147, bf16[3072,1152]{1,0:T(8,128)(2,1)} %param.13, f32[1152]{0:T(1024)} %param.14), kind=kOutput, calls=%fused_computation.24 | convolution fusion | flops 1812234240 | bytes 9835008 | tf_op jit(solution)/shard_map/dot_general | solution.py:25
  13.0 1.4 %copy.74 = f32[256,1152]{0,1:T(8,128)} copy(f32[256,1152]{1,0:T(8,128)S(1)} %convolution_add_fusion) | data formatting | bytes 2359296 | tf_op jit(solution)/shard_map/add | solution.py:25
  14.4 1.9 %reshape.48 = f32[2,128,3,3,128]{1,0,4,3,2:T(2,128)S(1)} reshape(f32[256,1152]{0,1:T(8,128)} %copy.74) | data formatting | bytes 2359296 | tf_op jit(solution)/shard_map/reshape | solution.py:26
  16.3 0.0 copy-start.11
  16.3 0.9 multiply_reduce_fusion
  17.2 1.8 %slice_reduce_fusion = (f32[2,3,128]{0,2,1:T(8,128)}, f32[2,128,1,3,128]{1,0,4,3,2:T(2,128)}) fusion(f32[2,128,3,3,128]{1,0,4,3,2:T(2,128)S(1)} %reshape.48), kind=kLoop, calls=%fused_computation.65 | loop fusion | flops 97536 | bytes 789504 | tf_op jit(solution)/shard_map/reduce_sum | solution.py:38
  18.9 1.9 %copy.98 = f32[2,128,1,3,128]{4,1,3,0,2:T(8,128)} copy(f32[2,128,1,3,128]{1,0,4,3,2:T(2,128)} %get-tuple-element.139) | data formatting | bytes 786432
  20.9 0.8 copy.80
  21.7 0.7 add_rsqrt_fusion
  22.4 0.0 copy-start.1
  22.4 0.0 copy-start.5
  22.5 2.6 %fusion.33 = (f32[2,3,128]{0,2,1:T(8,128)}, f32[2,128,3,128]{1,0,3,2:T(2,128)S(1)}, f32[2,3,128,128]{2,0,3,1:T(2,128)}) fusion(f32[128]{0:T(128)} %param.16, f32[2,128,3]{1,0,2:T(2,128)S(1)} %get-tuple-element.149, f32[2,128,3,3,128]{1,0,4,3,2:T(2,128)S(1)} %reshape.48, f32[128]{0:T(128)} %param.15, f32[2,128,3]{1,0,2:T(2,128)S(1)} %get-tuple-element.150), kind=kLoop, calls=%fused_computation.66 | loop fusion | flops 490752 | bytes 1583104 | tf_op jit(solution)/shard_map/reduce_sum | solution.py:38
  25.0 0.5 broadcast_subtract_fusion
  25.5 0.3 fusion.15
  25.9 0.5 fusion.16
  26.4 0.6 copy.84
  27.1 0.0 all-gather.3.cloned.1.call-update
  27.1 1.2 %copy.75 = f32[2,3,128,128]{3,2,1,0:T(8,128)S(1)} copy(f32[2,3,128,128]{2,0,3,1:T(2,128)} %get-tuple-element.140) | data formatting | bytes 786432 | tf_op jit(solution)/shard_map/transpose | solution.py:42
  28.3 1.6 %copy.88 = f32[2,1,3,128]{3,1,2,0:T(1,128)} copy(f32[2,1,3,128]{0,3,2,1:T(8,128)} %bitcast.141) | data formatting | bytes 6144 | tf_op jit(solution)/shard_map/stack | solution.py:38
  29.9 1.0 copy.101
  31.0 0.7 pad_maximum_fusion
  31.7 25.1 %all-gather = f32[32,2,3,128]{3,1,2,0:T(2,128)} all-gather(f32[2,2,3,128]{3,1,2,0:T(2,128)S(1)} %pad_maximum_fusion), channel_id=2, replica_groups=mesh['groups'=2,'seq'=16] {'seq'}, dimensions={0}, use_global_device_ids=true | all-gather | bytes 104448 | tf_op jit(solution)/shard_map/all_gather | solution.py:39
  56.7 0.9 reduce.1
  57.7 0.7 broadcast_compare_fusion
  58.4 0.8 fusion.32
  59.1 0.6 copy.92
  59.7 0.6 fusion.31
  60.3 0.8 fusion.37
  61.1 0.1 fusion.22
  61.2 0.8 fusion.17
  62.1 6.7 %all-gather.3.cloned.1.call-done = bf16[2048,384]{0,1:T(8,128)(2,1)} async-done(((bf16[128,384]{0,1:T(8,128)(2,1)}), bf16[2048,384]{0,1:T(8,128)(2,1)}) %all-gather.3.cloned.1.call-update) | async-done | bytes 1572880 | tf_op jit(solution)/shard_map/all_gather | solution.py:79
  68.8 3.8 %reshape_reshape.7 = bf16[4,512,2,2,3,32]{1,0,5,4,3,2:T(4,128)(2,1)} reshape(bf16[2048,384]{0,1:T(8,128)(2,1)} %all-gather.3.cloned.1.call-done) | data formatting | bytes 3145728 | tf_op jit(solution)/shard_map/reshape;reshape | solution.py:91
  72.6 2.9 %copy.85 = bf16[4,512,2,2,3,32]{1,5,4,2,3,0:T(8,128)(2,1)} copy(bf16[4,512,2,2,3,32]{1,0,5,4,3,2:T(4,128)(2,1)} %reshape_reshape.7) | data formatting | bytes 3145728 | tf_op jit(solution)/shard_map/while | solution.py:94
  75.6 0.0 copy-done.8
  75.6 30.7 %while.14 = (s32[]{:T(128)}, f32[2,3,128]{2,1,0:T(4,128)S(1)}, f32[2,3,128]{2,1,0:T(4,128)S(1)}, f32[2,3,128,128]{3,2,1,0:T(8,128)S(1)}, pred[4,512]{1,0:T(4,128...) while((s32[]{:T(128)}, f32[2,3,128]{2,1,0:T(4,128)S(1)}, ...), condition=%wide.region_7.8_spmd, body=%wide.region_4.7_spmd.sunk | while | flops 1513293312 | bytes 13524605 | solution.py:94
  75.6 1.0 dynamic-slice_bitcast_fusion.2
  76.6 0.9 fusion.55
  77.6 1.6 %bitcast_reduce_fusion.2 = (f32[2,3,128]{2,1,0:T(4,128)S(1)}, f32[2,3,512,128]{3,2,1,0:T(8,128)S(1)}) fusion(f32[2,3,128,128]{3,2,1,0:T(8,128)S(1)} %get-tuple-element.260, f32[3,512,2,128]{3,1,0,2:T(8,128)S(1)} %fusion.55, f32[2,3,128]{2,1,0:T(4,128)S(1)} %bitcast.145, pred[512]{0:T(512)(128)(4,1)S(1)} %dynamic-slice_reduce_fusion.2), kind=kOutput, calls=%fused_computation.3.clone.1 | convolution fusion | flops 605551872 | bytes 3545600 | tf_op jit(solution)/shard_map/while/body/eval_jaxpr/bhqd,bhsd->bhqs/dot_general | solution.py:64
  79.2 0.2 fusion.56
  79.5 0.9 fusion.57
  80.4 2.9 %fusion.58 = f32[2,3,128,128]{3,2,1,0:T(8,128)S(1)} fusion(f32[3,512,2,128]{3,1,0,2:T(8,128)S(1)} %fusion.57, f32[2,3,512,128]{3,2,1,0:T(8,128)S(1)} %get-tuple-element.225, f32[2,3,128]{2,1,0:T(4,128)S(1)} %bitcast.144, f32[2,3,128]{2,1,0:T(4,128)S(1)} %max.4, f32[2,3,128,128]{3,2,1,0:T(8,128)S(1)} %get-tuple-element.243, ...), kind=kOutput, calls=%fused_computation.9.clone.1 | convolution fusion | flops 604962816 | bytes 3941376 | tf_op jit(solution)/shard_map/while/body/eval_jaxpr/bhqs,bhsd->bhqd/dot_general | solution.py:74
  83.3 1.0 dynamic-slice_bitcast_fusion.2
  84.3 0.9 fusion.55
  85.2 1.6 %bitcast_reduce_fusion.2 = (f32[2,3,128]{2,1,0:T(4,128)S(1)}, f32[2,3,512,128]{3,2,1,0:T(8,128)S(1)}) fusion(f32[2,3,128,128]{3,2,1,0:T(8,128)S(1)} %get-tuple-element.260, f32[3,512,2,128]{3,1,0,2:T(8,128)S(1)} %fusion.55, f32[2,3,128]{2,1,0:T(4,128)S(1)} %bitcast.145, pred[512]{0:T(512)(128)(4,1)S(1)} %dynamic-slice_reduce_fusion.2), kind=kOutput, calls=%fused_computation.3.clone.1 | convolution fusion | flops 605551872 | bytes 3545600 | tf_op jit(solution)/shard_map/while/body/eval_jaxpr/bhqd,bhsd->bhqs/dot_general | solution.py:64
  86.9 0.2 fusion.56
  87.1 0.9 fusion.57
  88.1 2.9 %fusion.58 = f32[2,3,128,128]{3,2,1,0:T(8,128)S(1)} fusion(f32[3,512,2,128]{3,1,0,2:T(8,128)S(1)} %fusion.57, f32[2,3,512,128]{3,2,1,0:T(8,128)S(1)} %get-tuple-element.225, f32[2,3,128]{2,1,0:T(4,128)S(1)} %bitcast.144, f32[2,3,128]{2,1,0:T(4,128)S(1)} %max.4, f32[2,3,128,128]{3,2,1,0:T(8,128)S(1)} %get-tuple-element.243, ...), kind=kOutput, calls=%fused_computation.9.clone.1 | convolution fusion | flops 604962816 | bytes 3941376 | tf_op jit(solution)/shard_map/while/body/eval_jaxpr/bhqs,bhsd->bhqd/dot_general | solution.py:74
  91.0 1.0 dynamic-slice_bitcast_fusion.2
  92.0 0.9 fusion.55
  92.9 1.6 %bitcast_reduce_fusion.2 = (f32[2,3,128]{2,1,0:T(4,128)S(1)}, f32[2,3,512,128]{3,2,1,0:T(8,128)S(1)}) fusion(f32[2,3,128,128]{3,2,1,0:T(8,128)S(1)} %get-tuple-element.260, f32[3,512,2,128]{3,1,0,2:T(8,128)S(1)} %fusion.55, f32[2,3,128]{2,1,0:T(4,128)S(1)} %bitcast.145, pred[512]{0:T(512)(128)(4,1)S(1)} %dynamic-slice_reduce_fusion.2), kind=kOutput, calls=%fused_computation.3.clone.1 | convolution fusion | flops 605551872 | bytes 3545600 | tf_op jit(solution)/shard_map/while/body/eval_jaxpr/bhqd,bhsd->bhqs/dot_general | solution.py:64
  94.6 0.2 fusion.56
  94.8 0.9 fusion.57
  95.7 2.9 %fusion.58 = f32[2,3,128,128]{3,2,1,0:T(8,128)S(1)} fusion(f32[3,512,2,128]{3,1,0,2:T(8,128)S(1)} %fusion.57, f32[2,3,512,128]{3,2,1,0:T(8,128)S(1)} %get-tuple-element.225, f32[2,3,128]{2,1,0:T(4,128)S(1)} %bitcast.144, f32[2,3,128]{2,1,0:T(4,128)S(1)} %max.4, f32[2,3,128,128]{3,2,1,0:T(8,128)S(1)} %get-tuple-element.243, ...), kind=kOutput, calls=%fused_computation.9.clone.1 | convolution fusion | flops 604962816 | bytes 3941376 | tf_op jit(solution)/shard_map/while/body/eval_jaxpr/bhqs,bhsd->bhqd/dot_general | solution.py:74
  98.6 1.0 dynamic-slice_bitcast_fusion.2
  99.7 0.9 fusion.55
  100.6 1.6 %bitcast_reduce_fusion.2 = (f32[2,3,128]{2,1,0:T(4,128)S(1)}, f32[2,3,512,128]{3,2,1,0:T(8,128)S(1)}) fusion(f32[2,3,128,128]{3,2,1,0:T(8,128)S(1)} %get-tuple-element.260, f32[3,512,2,128]{3,1,0,2:T(8,128)S(1)} %fusion.55, f32[2,3,128]{2,1,0:T(4,128)S(1)} %bitcast.145, pred[512]{0:T(512)(128)(4,1)S(1)} %dynamic-slice_reduce_fusion.2), kind=kOutput, calls=%fused_computation.3.clone.1 | convolution fusion | flops 605551872 | bytes 3545600 | tf_op jit(solution)/shard_map/while/body/eval_jaxpr/bhqd,bhsd->bhqs/dot_general | solution.py:64
  102.3 0.2 fusion.56
  102.5 0.9 fusion.57
  103.4 2.9 %fusion.58 = f32[2,3,128,128]{3,2,1,0:T(8,128)S(1)} fusion(f32[3,512,2,128]{3,1,0,2:T(8,128)S(1)} %fusion.57, f32[2,3,512,128]{3,2,1,0:T(8,128)S(1)} %get-tuple-element.225, f32[2,3,128]{2,1,0:T(4,128)S(1)} %bitcast.144, f32[2,3,128]{2,1,0:T(4,128)S(1)} %max.4, f32[2,3,128,128]{3,2,1,0:T(8,128)S(1)} %get-tuple-element.243, ...), kind=kOutput, calls=%fused_computation.9.clone.1 | convolution fusion | flops 604962816 | bytes 3941376 | tf_op jit(solution)/shard_map/while/body/eval_jaxpr/bhqs,bhsd->bhqd/dot_general | solution.py:74
  106.3 0.2 fusion.26
  106.5 0.2 copy.87
  106.7 2.2 %convolution_convert_fusion = bf16[256,3072]{1,0:T(8,128)(2,1)} fusion(bf16[384,3072]{1,0:T(8,128)(2,1)S(1)} %copy-done, bf16[48,8,2,128]{3,2,1,0:T(2,128)(2,1)S(1)} %bitcast.140), kind=kOutput, calls=%fused_computation.23 | convolution fusion | flops 604766208 | bytes 4128768 | tf_op jit(solution)/shard_map/dot_general | solution.py:100
  (39 shorter events, 0.3 us)
Async XLA Ops:
  7.2 99.5 %copy-start = (bf16[384,3072]{1,0:T(8,128)(2,1)S(1)}, bf16[384,3072]{1,0:T(8,128)(2,1)}, u32[]{:S(2)}) copy-start(bf16[384,3072]{1,0:T(8,128)(2,1)} %param.21) | copy-start | bytes 7077892
  7.2 61.6 %all-gather.3.cloned.1.call-start = ((), (), s32[]{:S(2)}) async-start(), calls=%async_computation | async-start | bytes 1671168 | tf_op jit(solution)/shard_map/all_gather | solution.py:79
  16.3 4.6 %copy-start.11 = (f32[2,2,3,128]{3,1,2,0:T(2,128)S(1)}, f32[2,2,3,128]{3,1,2,0:T(2,128)}, u32[]{:S(2)}) copy-start(f32[2,2,3,128]{3,1,2,0:T(2,128)} %param.19) | copy-start | bytes 18436
  21.7 3.3 %copy-start.9 = (f32[2,3,128]{0,2,1:T(8,128)S(1)}, f32[2,3,128]{0,2,1:T(8,128)}, u32[]{:S(2)}) copy-start(f32[2,3,128]{0,2,1:T(8,128)} %copy.80) | copy-start | bytes 9220
  21.7 3.8 %copy-start.7 = (f32[3,128,32]{1,2,0:T(8,128)S(1)}, f32[3,128,32]{1,2,0:T(8,128)}, u32[]{:S(2)}) copy-start(f32[3,128,32]{1,2,0:T(8,128)} %param.17) | copy-start | bytes 147460
  22.4 3.4 %copy-start.1 = (f32[2,128,1,3,128]{4,1,3,0,2:T(8,128)S(1)}, f32[2,128,1,3,128]{4,1,3,0,2:T(8,128)}, u32[]{:S(2)}) copy-start(f32[2,128,1,3,128]{4,1,3,0,2:T(8,128)} %copy.98) | copy-start | bytes 1179652
  22.4 3.4 %copy-start.5 = (f32[3,128,32]{1,2,0:T(8,128)S(1)}, f32[3,128,32]{1,2,0:T(8,128)}, u32[]{:S(2)}) copy-start(f32[3,128,32]{1,2,0:T(8,128)} %param.18) | copy-start | bytes 147460
  25.0 1.4 %copy-start.3 = (f32[2,128,3,128]{1,0,3,2:T(2,128)}, f32[2,128,3,128]{1,0,3,2:T(2,128)S(1)}, u32[]{:S(2)}) copy-start(f32[2,128,3,128]{1,0,3,2:T(2,128)S(1)} %get-tuple-element.135) | copy-start | bytes 1179652
  26.4 33.9 %copy-start.4 = (f32[2,128,3,128]{1,0,3,2:T(2,128)S(1)}, f32[2,128,3,128]{1,0,3,2:T(2,128)}, u32[]{:S(2)}) copy-start(f32[2,128,3,128]{1,0,3,2:T(2,128)} %copy-done.3) | copy-start | bytes 1179652
  27.1 34.2 %copy-start.2 = (f32[2,128,1,3,128]{4,1,3,0,2:T(8,128)S(1)}, f32[2,128,1,3,128]{4,1,3,0,2:T(8,128)}, u32[]{:S(2)}) copy-start(f32[2,128,1,3,128]{4,1,3,0,2:T(8,128)} %copy.98) | copy-start | bytes 1179652
  72.6 2.9 %copy-start.6 = (f32[3,128,32]{1,2,0:T(8,128)S(1)}, f32[3,128,32]{1,2,0:T(8,128)}, u32[]{:S(2)}) copy-start(f32[3,128,32]{1,2,0:T(8,128)} %param.18) | copy-start | bytes 147460
  72.6 2.9 %copy-start.8 = (f32[3,128,32]{1,2,0:T(8,128)S(1)}, f32[3,128,32]{1,2,0:T(8,128)}, u32[]{:S(2)}) copy-start(f32[3,128,32]{1,2,0:T(8,128)} %param.17) | copy-start | bytes 147460
  72.6 2.9 %copy-start.10 = (pred[4,512]{1,0:T(4,128)(4,1)S(1)}, pred[4,512]{1,0:T(4,128)(4,1)}, u32[]{:S(2)}) copy-start(pred[4,512]{1,0:T(4,128)(4,1)} %fusion.31) | copy-start | bytes 6148
Sparse Core Ops, SparseCore 0:
  27.2 41.5 all-gather.2
